TPU v7x, 32 devices: a whole 2x2x4 slice. The times are simulated.
32 devices in a mesh: group: 4 (over y, core), member: 8 (over z, x).
Axes of the slice: x: 2, y: 2, z: 4, core: 2. Of those that a mesh axis runs over, the one named last changes fastest.
Arguments:
- features: bfloat16 [16384, 128], P(('group', 'member')), may hold values from -6 to 6
- edge_tiles: bfloat16 [8192, 128, 128], P(('group', 'member')), may hold values from -0.09375 to 0.09375
- tile_slot: int32 [32, 256], P(('group', 'member')), may hold values from 0 to 7
- tile_column: int32 [32, 256], P(('group', 'member')), may hold values from 0 to 31
- mirror_count: int32 [32, 4], P(('group', 'member')), may hold values from 0 to 2, as said below
- mirror_block: int32 [32, 4, 2], P(('group', 'member')), may hold values from 0 to 3, as said below
- weight_first: bfloat16 [128, 256], replicated, may hold values from -0.5 to 0.5
- bias_first: float32 [256], replicated, may hold values from -3 to 3
- weight_second: bfloat16 [256, 256], replicated, may hold values from -0.375 to 0.375
- bias_second: float32 [256], replicated, may hold values from -3 to 3
Outputs:
- layer_out: bfloat16 [16384, 256], P(('group', 'member'))
Inputs may be any that keep to these rules, and one draw needn't show every extreme that they name: `mirror_count`: at most 2 live mirror slots of one device for one destination group. `mirror_block`: the 2 entries of one device and destination group are distinct.
All inputs are finite; a program needn't handle non-finite values.
Results may differ from a plain program's by a relative error of at most 0.01.
Values may be sent and summed in bfloat16 or wider, within the bound.
A program may use at most 64 MiB of HBM per device.

v0:
```python
import math

import jax
import jax.numpy as jnp
from jax import lax
from jax.sharding import PartitionSpec as P


def expand(owners, block_count):
    return (owners[..., None] == jnp.arange(block_count)[None, None, :]).astype(jnp.bfloat16)


def fold_tiles(sources, edge_tiles, slot_ids, column_ids, alive_mask, slot_total):
    tile_total = edge_tiles.shape[0]
    tile_size = edge_tiles.shape[1]
    channels = sources.shape[2]
    block_tiles = math.gcd(tile_total, 32)
    rounds = tile_total // block_tiles
    tile_sets = edge_tiles.reshape(rounds, block_tiles, tile_size, tile_size)
    slot_sets = slot_ids.reshape(rounds, block_tiles)
    column_sets = column_ids.reshape(rounds, block_tiles)
    alive_sets = alive_mask.astype(jnp.float32).reshape(rounds, block_tiles)

    def advance(totals, pieces):
        tile_set, column_set, slot_set, alive_set = pieces
        source = jnp.take(sources, column_set, axis=0)
        products = jnp.einsum("tij,tjf->tif", tile_set, source, preferred_element_type=jnp.float32)
        return (totals.at[slot_set].add(products * alive_set[:, None, None]), None)

    start = jnp.zeros((slot_total, tile_size, channels), jnp.float32)
    totals, _ = lax.scan(advance, start, (tile_sets, column_sets, slot_sets, alive_sets))
    return totals.astype(jnp.bfloat16)


def body(
    features,
    edge_tiles,
    tile_slot,
    tile_column,
    mirror_count,
    mirror_block,
    weight_first,
    bias_first,
    weight_second,
    bias_second,
):
    group_count = lax.axis_size("group")
    slot_room = mirror_block.shape[2]
    tile_size = edge_tiles.shape[1]
    block_count = features.shape[0] // tile_size
    slot_ids = tile_slot[0]
    column_ids = tile_column[0]
    counts = mirror_count[0]
    targets = mirror_block[0]
    dest_group = slot_ids // slot_room
    within = slot_ids % slot_room
    count_of = jnp.sum(
        jnp.where(dest_group[:, None] == jnp.arange(group_count)[None, :], counts[None, :], 0),
        axis=1,
    )
    alive_mask = within < count_of
    spread = expand(targets, block_count)
    slot_total = group_count * slot_room

    def reduce_rows(partials):
        channels = partials.shape[2]
        spread_sums = jnp.einsum(
            "gcb,gcif->gbif",
            spread,
            partials.reshape(group_count, slot_room, tile_size, channels),
            preferred_element_type=jnp.float32,
        )
        return lax.psum_scatter(
            spread_sums.reshape(group_count * block_count, tile_size, channels).astype(
                jnp.bfloat16
            ),
            "group",
            scatter_dimension=0,
            tiled=True,
        ).astype(jnp.float32)

    local_rows = features.reshape(block_count, tile_size, features.shape[1])
    gathered = lax.all_gather(local_rows, "member", axis=0, tiled=True)
    first_sum = reduce_rows(
        fold_tiles(gathered, edge_tiles, slot_ids, column_ids, alive_mask, slot_total)
    ).astype(jnp.bfloat16)
    flat = first_sum.reshape(-1, first_sum.shape[2])
    result = jnp.maximum(
        jnp.dot(flat, weight_first, preferred_element_type=jnp.float32) + bias_first, 0.0
    )
    hidden = result.astype(jnp.bfloat16).reshape(first_sum.shape[0], tile_size, -1)
    sources = lax.all_gather(hidden, "member", axis=0, tiled=True)
    second = reduce_rows(
        fold_tiles(sources, edge_tiles, slot_ids, column_ids, alive_mask, slot_total)
    ).astype(jnp.bfloat16)
    flat_second = second.reshape(block_count * tile_size, -1)
    return (
        jnp.dot(flat_second, weight_second, preferred_element_type=jnp.float32) + bias_second
    ).astype(jnp.bfloat16)


def solution(mesh):
    placed = (
        P(("group", "member"), None),
        P(("group", "member"), None, None),
        P(("group", "member"), None),
        P(("group", "member"), None),
        P(("group", "member"), None),
        P(("group", "member"), None, None),
        P(),
        P(),
        P(),
        P(),
    )
    return jax.shard_map(
        body, mesh=mesh, in_specs=placed, out_specs=P(("group", "member"), None), check_vma=False
    )
```

profile of v0, /device:TPU:31, one launch (start us, length us, event | category | flops | bytes accessed | tf_op | source)
XLA Modules:
  0.0 322.1 jit_solution(12725843926485415464)
XLA Ops:
  13.1 33.5 %all-gather.3.cloned.1.call-done = bf16[32,128,128]{2,1,0:T(8,128)(2,1)} async-done(((bf16[4,128,128]{2,1,0:T(8,128)(2,1)}), bf16[32,128,128]{2,1,0:T(8,128)(2,1)}) %all-gather.3.cloned.1.call-update) | async-done | bytes 1048592 | tf_op jit(solution)/shard_map/all_gather | solution.py:83
  46.7 62.0 %while.20 = (s32[]{:T(128)}, f32[8,128,128]{2,1,0:T(8,128)S(1)}, s32[8,32]{1,0:T(8,128)S(1)}, bf16[8,32,128,128]{3,2,1,0:T(8,128)(2,1)}, s32[8,32]{1,0:T(8,128)S...) while((s32[]{:T(128)}, f32[8,128,128]{2,1,0:T(8,128)S(1)}, s32[8,32]{1,0:T(8,128)S(1)}, ...), condition=%wide.region_3.4_spmd, body=%wide.region_1.3_spmd.sunk | while | flops 135792000 | bytes 12589089 | solution.py:31
  46.7 2.9 gather_fusion
  51.7 2.7 scatter_fusion
  54.4 2.9 gather_fusion
  59.5 2.7 scatter_fusion
  62.2 2.9 gather_fusion
  67.2 2.7 scatter_fusion
  69.9 2.9 gather_fusion
  72.9 2.1 convolution_multiply_fusion.4
  75.0 2.7 scatter_fusion
  77.7 2.9 gather_fusion
  82.7 2.7 scatter_fusion
  85.4 2.9 gather_fusion
  88.4 2.1 convolution_multiply_fusion.4
  90.5 2.7 scatter_fusion
  93.2 2.9 gather_fusion
  98.2 2.7 scatter_fusion
  100.9 2.9 gather_fusion
  106.0 2.7 scatter_fusion
  110.3 23.6 %reduce-scatter.3.cloned.1.call-done = bf16[4,128,128]{2,1,0:T(8,128)(2,1)} async-done(((bf16[16,128,128]{2,1,0:T(8,128)(2,1)}), bf16[4,128,128]{2,1,0:T(8,128)(2,1)}) %reduce-scatter.3.cloned.1.call-update) | async-done | bytes 131088 | tf_op jit(solution)/shard_map/reduce_scatter | solution.py:73
  135.7 48.2 %all-gather.5.cloned.1.call-done = bf16[32,128,256]{2,1,0:T(8,128)(2,1)} async-done(((bf16[4,128,256]{2,1,0:T(8,128)(2,1)}), bf16[32,128,256]{2,1,0:T(8,128)(2,1)}) %all-gather.5.cloned.1.call-update) | async-done | bytes 2097168 | tf_op jit(solution)/shard_map/all_gather | solution.py:92
  184.0 102.0 %while.21 = (s32[]{:T(128)}, f32[8,128,256]{2,1,0:T(8,128)S(1)}, s32[8,32]{1,0:T(8,128)S(1)}, bf16[8,32,128,128]{3,2,1,0:T(8,128)(2,1)}, s32[8,32]{1,0:T(8,128)S...) while((s32[]{:T(128)}, f32[8,128,256]{2,1,0:T(8,128)S(1)}, s32[8,32]{1,0:T(8,128)S(1)}, ...), condition=%wide.region_7.8_spmd, body=%wide.region_5.7_spmd.sunk | while | flops 271582592 | bytes 24123424 | solution.py:31
  184.1 2.3 gather_fusion.1
  186.4 3.9 %convolution_multiply_fusion.5 = f32[32,128,256]{2,1,0:T(8,128)} fusion(f32[32]{0:T(128)S(1)} %fusion.53, bf16[32,128,256]{2,1,0:T(8,128)(2,1)S(1)} %gather_fusion.1, pred[32]{0:T(512)(128)(4,1)S(1)} %compare_and_fusion.5, bf16[8,32,128,128]{3,2,1,0:T(8,128)(2,1)} %get-tuple-element.250, s32[]{:T(128)} %get-tuple-element.239), kind=kOutput, calls=%fused_computation.24.clone.1 | convolution fusion | flops 270532608 | bytes 7340704 | tf_op jit(solution)/shard_map/while/body/eval_jaxpr/tij,tjf->tif/dot_general | solution.py:27
  190.3 6.5 %scatter_fusion.1 = f32[8,128,256]{2,1,0:T(8,128)S(1)} fusion(f32[8,128,256]{2,1,0:T(8,128)S(1)} %get-tuple-element.240, s32[32]{0:T(128)S(1)} %get-tuple-element.205, f32[32,128,256]{2,1,0:T(8,128)} %convolution_multiply_fusion.5), kind=kCustom, calls=%fused_computation.3.clone.1 | custom fusion | flops 1048576 | bytes 12583040 | tf_op jit(solution)/shard_map/while/body/eval_jaxpr/scatter-add | solution.py:28
  196.8 2.3 gather_fusion.1
  199.2 3.9 %convolution_multiply_fusion.5 = f32[32,128,256]{2,1,0:T(8,128)} fusion(f32[32]{0:T(128)S(1)} %fusion.53, bf16[32,128,256]{2,1,0:T(8,128)(2,1)S(1)} %gather_fusion.1, pred[32]{0:T(512)(128)(4,1)S(1)} %compare_and_fusion.5, bf16[8,32,128,128]{3,2,1,0:T(8,128)(2,1)} %get-tuple-element.250, s32[]{:T(128)} %get-tuple-element.239), kind=kOutput, calls=%fused_computation.24.clone.1 | convolution fusion | flops 270532608 | bytes 7340704 | tf_op jit(solution)/shard_map/while/body/eval_jaxpr/tij,tjf->tif/dot_general | solution.py:27
  203.1 6.4 %scatter_fusion.1 = f32[8,128,256]{2,1,0:T(8,128)S(1)} fusion(f32[8,128,256]{2,1,0:T(8,128)S(1)} %get-tuple-element.240, s32[32]{0:T(128)S(1)} %get-tuple-element.205, f32[32,128,256]{2,1,0:T(8,128)} %convolution_multiply_fusion.5), kind=kCustom, calls=%fused_computation.3.clone.1 | custom fusion | flops 1048576 | bytes 12583040 | tf_op jit(solution)/shard_map/while/body/eval_jaxpr/scatter-add | solution.py:28
  209.6 2.3 gather_fusion.1
  211.9 3.9 %convolution_multiply_fusion.5 = f32[32,128,256]{2,1,0:T(8,128)} fusion(f32[32]{0:T(128)S(1)} %fusion.53, bf16[32,128,256]{2,1,0:T(8,128)(2,1)S(1)} %gather_fusion.1, pred[32]{0:T(512)(128)(4,1)S(1)} %compare_and_fusion.5, bf16[8,32,128,128]{3,2,1,0:T(8,128)(2,1)} %get-tuple-element.250, s32[]{:T(128)} %get-tuple-element.239), kind=kOutput, calls=%fused_computation.24.clone.1 | convolution fusion | flops 270532608 | bytes 7340704 | tf_op jit(solution)/shard_map/while/body/eval_jaxpr/tij,tjf->tif/dot_general | solution.py:27
  215.8 6.4 %scatter_fusion.1 = f32[8,128,256]{2,1,0:T(8,128)S(1)} fusion(f32[8,128,256]{2,1,0:T(8,128)S(1)} %get-tuple-element.240, s32[32]{0:T(128)S(1)} %get-tuple-element.205, f32[32,128,256]{2,1,0:T(8,128)} %convolution_multiply_fusion.5), kind=kCustom, calls=%fused_computation.3.clone.1 | custom fusion | flops 1048576 | bytes 12583040 | tf_op jit(solution)/shard_map/while/body/eval_jaxpr/scatter-add | solution.py:28
  222.3 2.3 gather_fusion.1
  224.7 3.9 %convolution_multiply_fusion.5 = f32[32,128,256]{2,1,0:T(8,128)} fusion(f32[32]{0:T(128)S(1)} %fusion.53, bf16[32,128,256]{2,1,0:T(8,128)(2,1)S(1)} %gather_fusion.1, pred[32]{0:T(512)(128)(4,1)S(1)} %compare_and_fusion.5, bf16[8,32,128,128]{3,2,1,0:T(8,128)(2,1)} %get-tuple-element.250, s32[]{:T(128)} %get-tuple-element.239), kind=kOutput, calls=%fused_computation.24.clone.1 | convolution fusion | flops 270532608 | bytes 7340704 | tf_op jit(solution)/shard_map/while/body/eval_jaxpr/tij,tjf->tif/dot_general | solution.py:27
  228.6 6.5 %scatter_fusion.1 = f32[8,128,256]{2,1,0:T(8,128)S(1)} fusion(f32[8,128,256]{2,1,0:T(8,128)S(1)} %get-tuple-element.240, s32[32]{0:T(128)S(1)} %get-tuple-element.205, f32[32,128,256]{2,1,0:T(8,128)} %convolution_multiply_fusion.5), kind=kCustom, calls=%fused_computation.3.clone.1 | custom fusion | flops 1048576 | bytes 12583040 | tf_op jit(solution)/shard_map/while/body/eval_jaxpr/scatter-add | solution.py:28
  235.1 2.3 gather_fusion.1
  237.4 3.9 %convolution_multiply_fusion.5 = f32[32,128,256]{2,1,0:T(8,128)} fusion(f32[32]{0:T(128)S(1)} %fusion.53, bf16[32,128,256]{2,1,0:T(8,128)(2,1)S(1)} %gather_fusion.1, pred[32]{0:T(512)(128)(4,1)S(1)} %compare_and_fusion.5, bf16[8,32,128,128]{3,2,1,0:T(8,128)(2,1)} %get-tuple-element.250, s32[]{:T(128)} %get-tuple-element.239), kind=kOutput, calls=%fused_computation.24.clone.1 | convolution fusion | flops 270532608 | bytes 7340704 | tf_op jit(solution)/shard_map/while/body/eval_jaxpr/tij,tjf->tif/dot_general | solution.py:27
  241.3 6.5 %scatter_fusion.1 = f32[8,128,256]{2,1,0:T(8,128)S(1)} fusion(f32[8,128,256]{2,1,0:T(8,128)S(1)} %get-tuple-element.240, s32[32]{0:T(128)S(1)} %get-tuple-element.205, f32[32,128,256]{2,1,0:T(8,128)} %convolution_multiply_fusion.5), kind=kCustom, calls=%fused_computation.3.clone.1 | custom fusion | flops 1048576 | bytes 12583040 | tf_op jit(solution)/shard_map/while/body/eval_jaxpr/scatter-add | solution.py:28
  247.9 2.3 gather_fusion.1
  250.2 3.9 %convolution_multiply_fusion.5 = f32[32,128,256]{2,1,0:T(8,128)} fusion(f32[32]{0:T(128)S(1)} %fusion.53, bf16[32,128,256]{2,1,0:T(8,128)(2,1)S(1)} %gather_fusion.1, pred[32]{0:T(512)(128)(4,1)S(1)} %compare_and_fusion.5, bf16[8,32,128,128]{3,2,1,0:T(8,128)(2,1)} %get-tuple-element.250, s32[]{:T(128)} %get-tuple-element.239), kind=kOutput, calls=%fused_computation.24.clone.1 | convolution fusion | flops 270532608 | bytes 7340704 | tf_op jit(solution)/shard_map/while/body/eval_jaxpr/tij,tjf->tif/dot_general | solution.py:27
  254.1 6.4 %scatter_fusion.1 = f32[8,128,256]{2,1,0:T(8,128)S(1)} fusion(f32[8,128,256]{2,1,0:T(8,128)S(1)} %get-tuple-element.240, s32[32]{0:T(128)S(1)} %get-tuple-element.205, f32[32,128,256]{2,1,0:T(8,128)} %convolution_multiply_fusion.5), kind=kCustom, calls=%fused_computation.3.clone.1 | custom fusion | flops 1048576 | bytes 12583040 | tf_op jit(solution)/shard_map/while/body/eval_jaxpr/scatter-add | solution.py:28
  260.6 2.3 gather_fusion.1
  262.9 3.9 %convolution_multiply_fusion.5 = f32[32,128,256]{2,1,0:T(8,128)} fusion(f32[32]{0:T(128)S(1)} %fusion.53, bf16[32,128,256]{2,1,0:T(8,128)(2,1)S(1)} %gather_fusion.1, pred[32]{0:T(512)(128)(4,1)S(1)} %compare_and_fusion.5, bf16[8,32,128,128]{3,2,1,0:T(8,128)(2,1)} %get-tuple-element.250, s32[]{:T(128)} %get-tuple-element.239), kind=kOutput, calls=%fused_computation.24.clone.1 | convolution fusion | flops 270532608 | bytes 7340704 | tf_op jit(solution)/shard_map/while/body/eval_jaxpr/tij,tjf->tif/dot_general | solution.py:27
  266.9 6.4 %scatter_fusion.1 = f32[8,128,256]{2,1,0:T(8,128)S(1)} fusion(f32[8,128,256]{2,1,0:T(8,128)S(1)} %get-tuple-element.240, s32[32]{0:T(128)S(1)} %get-tuple-element.205, f32[32,128,256]{2,1,0:T(8,128)} %convolution_multiply_fusion.5), kind=kCustom, calls=%fused_computation.3.clone.1 | custom fusion | flops 1048576 | bytes 12583040 | tf_op jit(solution)/shard_map/while/body/eval_jaxpr/scatter-add | solution.py:28
  273.4 2.3 gather_fusion.1
  275.7 3.9 %convolution_multiply_fusion.5 = f32[32,128,256]{2,1,0:T(8,128)} fusion(f32[32]{0:T(128)S(1)} %fusion.53, bf16[32,128,256]{2,1,0:T(8,128)(2,1)S(1)} %gather_fusion.1, pred[32]{0:T(512)(128)(4,1)S(1)} %compare_and_fusion.5, bf16[8,32,128,128]{3,2,1,0:T(8,128)(2,1)} %get-tuple-element.250, s32[]{:T(128)} %get-tuple-element.239), kind=kOutput, calls=%fused_computation.24.clone.1 | convolution fusion | flops 270532608 | bytes 7340704 | tf_op jit(solution)/shard_map/while/body/eval_jaxpr/tij,tjf->tif/dot_general | solution.py:27
  279.6 6.5 %scatter_fusion.1 = f32[8,128,256]{2,1,0:T(8,128)S(1)} fusion(f32[8,128,256]{2,1,0:T(8,128)S(1)} %get-tuple-element.240, s32[32]{0:T(128)S(1)} %get-tuple-element.205, f32[32,128,256]{2,1,0:T(8,128)} %convolution_multiply_fusion.5), kind=kCustom, calls=%fused_computation.3.clone.1 | custom fusion | flops 1048576 | bytes 12583040 | tf_op jit(solution)/shard_map/while/body/eval_jaxpr/scatter-add | solution.py:28
  288.6 25.1 %reduce-scatter.5.cloned.1.call-done = bf16[4,128,256]{2,1,0:T(8,128)(2,1)} async-done(((bf16[16,128,256]{2,1,0:T(8,128)(2,1)}), bf16[4,128,256]{2,1,0:T(8,128)(2,1)}) %reduce-scatter.5.cloned.1.call-update) | async-done | bytes 262160 | tf_op jit(solution)/shard_map/reduce_scatter | solution.py:73
  (106 shorter events, 27.5 us)
Async XLA Ops:
  6.5 307.2 %copy-start = (bf16[256,256]{1,0:T(8,128)(2,1)S(1)}, bf16[256,256]{1,0:T(8,128)(2,1)}, u32[]{:S(2)}) copy-start(bf16[256,256]{1,0:T(8,128)(2,1)} %param.22) | copy-start | bytes 393220
  6.5 40.1 %all-gather.3.cloned.1.call-start = ((), (), s32[]{:S(2)}) async-start(), calls=%async_computation.2 | async-start | bytes 1179648 | tf_op jit(solution)/shard_map/all_gather | solution.py:83
  7.3 126.6 %reduce-scatter.3.cloned.1.call-start = ((), (), s32[]{:S(2)}) async-start(), calls=%async_computation.3 | async-start | bytes 655360 | tf_op jit(solution)/shard_map/reduce_scatter | solution.py:73
  108.6 25.2 %copy-start.1 = (bf16[128,256]{1,0:T(8,128)(2,1)S(1)}, bf16[128,256]{1,0:T(8,128)(2,1)}, u32[]{:S(2)}) copy-start(bf16[128,256]{1,0:T(8,128)(2,1)} %param.20) | copy-start | bytes 196612
  108.6 25.2 %copy-start.2 = (f32[256]{0:T(256)S(1)}, f32[256]{0:T(256)}, u32[]{:S(2)}) copy-start(f32[256]{0:T(256)} %param.21) | copy-start | bytes 3076
  110.2 73.7 %all-gather.5.cloned.1.call-start = ((), (), s32[]{:S(2)}) async-start(), calls=%async_computation.4 | async-start | bytes 2359296 | tf_op jit(solution)/shard_map/all_gather | solution.py:92
  135.7 178.0 %reduce-scatter.5.cloned.1.call-start = ((), (), s32[]{:S(2)}) async-start(), calls=%async_computation.5 | async-start | bytes 1310720 | tf_op jit(solution)/shard_map/reduce_scatter | solution.py:73
  287.4 26.3 %copy-start.3 = (f32[256]{0:T(256)S(1)}, f32[256]{0:T(256)}, u32[]{:S(2)}) copy-start(f32[256]{0:T(256)} %param.23) | copy-start | bytes 3076
Sparse Core Ops, SparseCore 0:
  9.5 37.0 all-gather.2
  110.3 23.4 reduce-scatter.2
  136.2 47.7 all-gather.4
  288.7 24.9 reduce-scatter.4
where the time goes:
time: 327 us; the launch traced here: 322 us
  waiting for transfers between devices  131 us (40%)
  other arithmetic  77.7 us (24%)
  matrix products  53.4 us (16%)
  local copies, waits for them, and re-layouts  45.6 us (14%)
  between operations  13.2 us (4%)
    scatter-add x16, other arithmetic, advance(): return (totals.at[slot_set].add(products * alive_set[:, None, None]), None)  72.9 us
    reduce_scatter x2, waiting for transfers between devices, reduce_rows(): lax.psum_scatter(spread_sums.reshape(group_count * block_count, tile_size...  48.7 us
    all_gather x1, waiting for transfers between devices, body(): sources = lax.all_gather(hidden, 'member', axis=0, tiled=True)  48.2 us
    dot_general x16, matrix products, advance(): jnp.einsum('tij,tjf->tif', tile_set, source, preferred_element_type=jnp.f...  47.9 us
    gather x16, local copies, waits for them, and re-layouts, advance(): source = jnp.take(sources, column_set, axis=0)  41.7 us
    all_gather x1, waiting for transfers between devices, body(): gathered = lax.all_gather(local_rows, 'member', axis=0, tiled=True)  33.5 us
  transfers between devices with their start and end apart: 4, of which 4 were waited for; matrix products, arithmetic and copies ran while one was open for 2% of the time, Pallas kernels for 0%

commit v1 on v0

v1 whole, which is shorter than its diff:
```python
import functools

import jax
import jax.numpy as jnp
from jax import lax
from jax.experimental import pallas as pl
from jax.experimental.pallas import tpu as pltpu
from jax.sharding import PartitionSpec as P

F32 = jnp.float32
BF16 = jnp.bfloat16


def kernel(
    n,
    groups,
    cap,
    keep,
    prev_ref,
    last_ref,
    feat_ref,
    tiles_ref,
    hot_ref,
    w1_ref,
    b1_ref,
    w2_ref,
    b2_ref,
    out_ref,
    tile_buf,
    run_buf,
    stage_buf,
    gather1,
    gather2,
    acc1,
    acc2,
    part1,
    part2,
    got1,
    got2,
    got_hot,
    own_sum,
    tile_sem,
    hot_send,
    hot_recv,
    ag1_send,
    ag1_recv,
    rs1_send,
    rs1_recv,
    ag2_send,
    ag2_recv,
    rs2_send,
    rs2_recv,
):
    me = lax.axis_index("member")
    g = lax.axis_index("group")
    total = tiles_ref.shape[0]
    size = tiles_ref.shape[1]
    rows = feat_ref.shape[0]
    blocks = rows // size
    slots = groups * cap
    columns = n * blocks
    pieces = tile_sem.shape[0]
    piece = total // pieces

    def tile_copy(i):
        span = pl.ds(i * piece, piece)
        return pltpu.make_async_copy(tiles_ref.at[span], tile_buf.at[span], tile_sem.at[i])

    def member_copy(src, bank, k, send, recv):
        return pltpu.make_async_remote_copy(
            src_ref=src,
            dst_ref=bank.at[me],
            send_sem=send.at[k],
            recv_sem=recv.at[k],
            device_id={"member": lax.rem(me + k, n)},
            device_id_type=pl.DeviceIdType.MESH,
        )

    def member_arrival(src, bank, k, send, recv):
        origin = lax.rem(me + n - k, n)
        return pltpu.make_async_remote_copy(
            src_ref=src,
            dst_ref=bank.at[origin],
            send_sem=send.at[k],
            recv_sem=recv.at[k],
            device_id={"member": lax.rem(me + k, n)},
            device_id_type=pl.DeviceIdType.MESH,
        )

    def group_copy(bank, got, k, send, recv):
        to = lax.rem(g + k, groups)
        return pltpu.make_async_remote_copy(
            src_ref=bank.at[to],
            dst_ref=got.at[k],
            send_sem=send.at[k],
            recv_sem=recv.at[k],
            device_id={"group": to},
            device_id_type=pl.DeviceIdType.MESH,
        )

    for i in range(pieces):
        tile_copy(i).start()

    barrier = pltpu.get_barrier_semaphore()

    def greet_member(k, c):
        pl.semaphore_signal(
            barrier,
            inc=1,
            device_id={"member": lax.rem(me + k, n)},
            device_id_type=pl.DeviceIdType.MESH,
        )
        return c

    lax.fori_loop(1, n, greet_member, 0)
    for k in range(1, groups):
        pl.semaphore_signal(
            barrier,
            inc=1,
            device_id={"group": lax.rem(g + k, groups)},
            device_id_type=pl.DeviceIdType.MESH,
        )
    pl.semaphore_wait(barrier, n - 1 + groups - 1)

    def send_features(k, c):
        member_copy(feat_ref, gather1, k, ag1_send, ag1_recv).start()
        return c

    lax.fori_loop(1, n, send_features, 0)
    for k in range(1, groups):
        group_copy(hot_ref, got_hot, k, hot_send, hot_recv).start()

    gather1[me] = feat_ref[...]
    tile_buf[total] = jnp.zeros((size, size), BF16)
    run_buf[total] = jnp.zeros((size, size), F32)

    def chain(t, c):
        value = tile_buf[t].astype(F32) + run_buf[prev_ref[t]]
        run_buf[t] = value
        tile_buf[t] = value.astype(BF16)
        return c

    for i in range(pieces):
        tile_copy(i).wait()
        lax.fori_loop(i * piece, (i + 1) * piece, chain, 0)

    def stage(k, at):
        origin = lax.rem(me + n - k, n)
        for s in range(slots):
            for b in range(blocks):
                stage_buf[at, s * size : (s + 1) * size, b * size : (b + 1) * size] = tile_buf[
                    last_ref[s * columns + origin * blocks + b]
                ]

    if keep:

        def stage_all(k, c):
            stage(k, k)
            return c

        lax.fori_loop(0, n, stage_all, 0)

    def place(k):
        if keep:
            return k
        stage(k, 0)
        return 0

    def combine(part, got):
        sums = []
        for b in range(blocks):
            value = None
            for k in range(groups):
                hot = hot_ref[g] if k == 0 else got_hot[k]
                for c in range(cap):
                    block = (
                        part[g, c * size : (c + 1) * size, :]
                        if k == 0
                        else got[k, c * size : (c + 1) * size, :]
                    )
                    weight = hot[c * blocks + b : c * blocks + b + 1, :]
                    repeat = block.shape[1] // weight.shape[1]
                    if repeat > 1:
                        weight = jnp.concatenate([weight] * repeat, axis=1)
                    term = weight * block.astype(F32)
                    value = term if value is None else value + term
            sums.append(value.astype(BF16))
        return sums

    acc1[...] = jnp.dot(stage_buf[place(0)], feat_ref[...], preferred_element_type=F32)

    def first_layer(k, c):
        at = place(k)
        member_arrival(feat_ref, gather1, k, ag1_send, ag1_recv).wait_recv()
        origin = lax.rem(me + n - k, n)
        acc1[...] += jnp.dot(stage_buf[at], gather1[origin], preferred_element_type=F32)
        return c

    lax.fori_loop(1, n, first_layer, 0)
    for e in range(groups):
        part1[e] = acc1[e * cap * size : (e + 1) * cap * size, :].astype(BF16)
    for k in range(1, groups):
        group_copy(part1, got1, k, rs1_send, rs1_recv).start()
    for k in range(1, groups):
        group_copy(hot_ref, got_hot, k, hot_send, hot_recv).wait_recv()
    for k in range(1, groups):
        group_copy(part1, got1, k, rs1_send, rs1_recv).wait_recv()
    sums = combine(part1, got1)
    for b in range(blocks):
        own_sum[b * size : (b + 1) * size, :] = sums[b]

    def send_sums(k, c):
        member_copy(own_sum, gather2, k, ag2_send, ag2_recv).start()
        return c

    lax.fori_loop(1, n, send_sums, 0)

    def hidden_of(value):
        raw = jnp.dot(value, w1_ref[...], preferred_element_type=F32) + b1_ref[...]
        return jnp.maximum(raw, 0.0).astype(BF16)

    acc2[...] = jnp.dot(stage_buf[place(0)], hidden_of(own_sum[...]), preferred_element_type=F32)

    def second_layer(k, c):
        at = place(k)
        member_arrival(own_sum, gather2, k, ag2_send, ag2_recv).wait_recv()
        origin = lax.rem(me + n - k, n)
        acc2[...] += jnp.dot(
            stage_buf[at], hidden_of(gather2[origin]), preferred_element_type=F32
        )
        return c

    lax.fori_loop(1, n, second_layer, 0)
    for e in range(groups):
        part2[e] = acc2[e * cap * size : (e + 1) * cap * size, :].astype(BF16)
    for k in range(1, groups):
        group_copy(part2, got2, k, rs2_send, rs2_recv).start()

    def drain(k, c):
        member_copy(feat_ref, gather1, k, ag1_send, ag1_recv).wait_send()
        member_copy(own_sum, gather2, k, ag2_send, ag2_recv).wait_send()
        return c

    lax.fori_loop(1, n, drain, 0)
    for k in range(1, groups):
        group_copy(hot_ref, got_hot, k, hot_send, hot_recv).wait_send()
        group_copy(part1, got1, k, rs1_send, rs1_recv).wait_send()
    for k in range(1, groups):
        group_copy(part2, got2, k, rs2_send, rs2_recv).wait_recv()
    sums = combine(part2, got2)
    for b in range(blocks):
        raw = jnp.dot(sums[b], w2_ref[...], preferred_element_type=F32) + b2_ref[...]
        out_ref[b * size : (b + 1) * size, :] = raw.astype(BF16)
    for k in range(1, groups):
        group_copy(part2, got2, k, rs2_send, rs2_recv).wait_send()


def body(
    features,
    edge_tiles,
    tile_slot,
    tile_column,
    mirror_count,
    mirror_block,
    weight_first,
    bias_first,
    weight_second,
    bias_second,
):
    groups = lax.axis_size("group")
    n = lax.axis_size("member")
    total, size, _ = edge_tiles.shape
    rows, width = features.shape
    hidden = weight_first.shape[1]
    outs = weight_second.shape[1]
    blocks = rows // size
    cap = mirror_block.shape[2]
    slots = groups * cap
    columns = n * blocks
    counts = mirror_count[0]
    slot = tile_slot[0]
    dest = slot // cap
    count_of = jnp.sum(
        jnp.where(dest[:, None] == jnp.arange(groups)[None, :], counts[None, :], 0), axis=1
    )
    live = (slot % cap) < count_of
    key = jnp.where(live, slot * columns + tile_column[0], -1)
    order = jnp.arange(total, dtype=jnp.int32)
    same = (key[:, None] == key[None, :]) & (order[None, :] < order[:, None])
    prev = jnp.max(jnp.where(same, order[None, :], -1), axis=1)
    prev = jnp.where(prev < 0, total, prev)
    combos = jnp.arange(slots * columns, dtype=jnp.int32)
    last = jnp.max(jnp.where(key[None, :] == combos[:, None], order[None, :], -1), axis=1)
    last = jnp.where(last < 0, total, last)
    hot = (mirror_block[0][:, :, None] == jnp.arange(blocks)[None, None, :]) & (
        jnp.arange(cap)[None, :, None] < counts[:, None, None]
    )
    hot = jnp.broadcast_to(
        hot.reshape(groups, cap * blocks, 1).astype(F32), (groups, cap * blocks, width)
    )
    keep = slots * columns <= 2 * total
    pieces = 8 if total % 8 == 0 else 1
    vmem = pl.BlockSpec(memory_space=pltpu.VMEM)
    smem = pl.BlockSpec(memory_space=pltpu.SMEM)
    dma = pltpu.SemaphoreType.DMA
    return pl.pallas_call(
        functools.partial(kernel, n, groups, cap, keep),
        out_shape=jax.ShapeDtypeStruct((rows, outs), BF16),
        in_specs=[smem, smem, vmem, pl.BlockSpec(memory_space=pl.ANY)] + [vmem] * 5,
        out_specs=vmem,
        scratch_shapes=[
            pltpu.VMEM((total + 1, size, size), BF16),
            pltpu.VMEM((total + 1, size, size), F32),
            pltpu.VMEM((n if keep else 1, slots * size, rows), BF16),
            pltpu.VMEM((n, rows, width), BF16),
            pltpu.VMEM((n, rows, width), BF16),
            pltpu.VMEM((slots * size, width), F32),
            pltpu.VMEM((slots * size, hidden), F32),
            pltpu.VMEM((groups, cap * size, width), BF16),
            pltpu.VMEM((groups, cap * size, hidden), BF16),
            pltpu.VMEM((groups, cap * size, width), BF16),
            pltpu.VMEM((groups, cap * size, hidden), BF16),
            pltpu.VMEM((groups, cap * blocks, width), F32),
            pltpu.VMEM((rows, width), BF16),
            dma((pieces,)),
            dma((groups,)),
            dma((groups,)),
            dma((n,)),
            dma((n,)),
            dma((groups,)),
            dma((groups,)),
            dma((n,)),
            dma((n,)),
            dma((groups,)),
            dma((groups,)),
        ],
        compiler_params=pltpu.CompilerParams(
            collective_id=0, has_side_effects=True, vmem_limit_bytes=56 * 1024 * 1024
        ),
    )(
        prev,
        last,
        features,
        edge_tiles,
        hot,
        weight_first,
        bias_first.reshape(1, -1),
        weight_second,
        bias_second.reshape(1, -1),
    )


def solution(mesh):
    placed = (
        P(("group", "member"), None),
        P(("group", "member"), None, None),
        P(("group", "member"), None),
        P(("group", "member"), None),
        P(("group", "member"), None),
        P(("group", "member"), None, None),
        P(),
        P(),
        P(),
        P(),
    )
    return jax.shard_map(
        body, mesh=mesh, in_specs=placed, out_specs=P(("group", "member"), None), check_vma=False
    )
```

time: 327 us -> 77 us (0.24); the launches traced: 322 us -> 76.7 us
  waiting for transfers between devices: 131 us -> 0 us
  other arithmetic: 77.7 us -> 4.3 us
  Pallas kernels: 0 us -> 69 us
  matrix products: 53.4 us -> 0 us
  local copies, waits for them, and re-layouts: 45.6 us -> 3.47 us
  between operations: 13.2 us -> 0.02 us
    all_gather x2 -> x0, waiting for transfers between devices: 81.7 us -> none  [the longest x1 48.2 us: body(): sources = lax.all_gather(hidden, 'member', axis=0, tiled=True)]
    scatter-add x16 -> x0, other arithmetic: 72.9 us -> none  [advance(): return (totals.at[slot_set].add(products * alive_set[:, None, None]), None)]
    pallas_call x0 -> x1, Pallas kernels: none -> 69 us  [body(): pl.pallas_call(functools.partial(kernel, n, groups, cap, keep), out_shape...]
    dot_general x20 -> x0, matrix products: 53.4 us -> none  [the longest x16 47.9 us: advance(): jnp.einsum('tij,tjf->tif', tile_set, source, preferred_element_type=jnp.f...]
    reduce_scatter x2 -> x0, waiting for transfers between devices: 48.7 us -> none  [reduce_rows(): lax.psum_scatter(spread_sums.reshape(group_count * block_count, tile_size...]
    gather x16 -> x0, local copies, waits for them, and re-layouts: 41.7 us -> none  [advance(): source = jnp.take(sources, column_set, axis=0)]
  transfers between devices with their start and end apart: 4 -> 0, of which waited for: 4 -> 0; matrix products, arithmetic and copies ran while one was open for 2% -> 0% of each run, Pallas kernels for 0% -> 0%
where the time goes in v1:
time: 77 us; the launch traced here: 76.7 us
  Pallas kernels  69 us (90%)
  other arithmetic  4.3 us (6%)
  local copies, waits for them, and re-layouts  3.47 us (5%)
    pallas_call x1, Pallas kernels, body(): pl.pallas_call(functools.partial(kernel, n, groups, cap, keep), out_shape...  69 us
    unnamed x1, local copies, waits for them, and re-layouts  1.67 us

profile of v1, /device:TPU:31, one launch (start us, length us, event | category | flops | bytes accessed | tf_op | source)
XLA Modules:
  0.0 76.7 jit_solution(14888977928691615704)
XLA Ops:
  0.0 0.7 iota_compare_fusion.3
  0.7 0.1 copy.14
  0.8 0.7 and_select_fusion.1
  1.5 0.7 select_reduce_fusion.2
  2.2 0.7 compare_select_fusion.4
  2.9 0.7 compare_select_fusion.5
  3.6 0.2 select_reduce_fusion
  3.8 0.6 compare_select_fusion.2
  4.4 0.1 eq.77
  4.5 0.8 copy.13
  5.3 0.1 eq.74
  5.3 0.1 eq.75
  5.4 0.7 broadcast_in_dim.60.hot_ref
  6.1 69.0 %shard_map.100 = bf16[512,256]{1,0:T(8,128)(2,1)} custom-call(s32[256]{0:T(256)} %get-tuple-element.8.prev_ref, s32[256]{0:T(256)} %get-tuple-element.7.last_ref, bf16[512,128]{1,0:T(8,128)(2,1)} %feat_ref.1, bf16[256,128,128]{2,1,0:T(8,128)(2,1)} %tiles_ref.1, f32[4,8,128]{2,1,0:T(8,128)} %broadcast_in_dim.60.hot_ref, bf16[128,256]{1,0:T(8,128)(2,1)} %w1_ref.1, ...), custom_call_target="tpu_custom_call" | custom-call | tf_op jit(solution)/shard_map/pallas_call | solution.py:306
  75.1 1.7 %copy.16 = bf16[512,256]{1,0:T(8,128)(2,1)} copy(bf16[512,256]{1,0:T(8,128)(2,1)} %shard_map.100) | data formatting | bytes 524288
  (3 shorter events, 0.0 us)

commit v2 on v1

--- a/solution.py
+++ b/solution.py
@@ -12,15 +12,17 @@
 
 
 def kernel(
-    n,
+    outer,
+    inner,
     groups,
     cap,
     keep,
-    prev_ref,
-    last_ref,
+    slot_ref,
+    column_ref,
+    count_ref,
+    mirror_ref,
     feat_ref,
     tiles_ref,
-    hot_ref,
     w1_ref,
     b1_ref,
     w2_ref,
@@ -39,6 +41,12 @@
     got2,
     got_hot,
     own_sum,
+    hot_ref,
+    prev_vmem,
+    last_vmem,
+    prev_ref,
+    last_ref,
+    table_sem,
     tile_sem,
     hot_send,
     hot_recv,
@@ -51,7 +59,9 @@
     rs2_send,
     rs2_recv,
 ):
+    n = outer * inner
     me = lax.axis_index("member")
+    me_outer, me_inner = me // inner, lax.rem(me, inner)
     g = lax.axis_index("group")
     total = tiles_ref.shape[0]
     size = tiles_ref.shape[1]
@@ -66,26 +76,69 @@
         span = pl.ds(i * piece, piece)
         return pltpu.make_async_copy(tiles_ref.at[span], tile_buf.at[span], tile_sem.at[i])
 
-    def member_copy(src, bank, k, send, recv):
+    def outer_copy(src, bank, j, send, recv, arriving=False):
+        from_outer = lax.rem(me_outer + outer - j, outer)
+        origin = from_outer * inner + me_inner
+        to = lax.rem(me_outer + j, outer) * inner + me_inner
         return pltpu.make_async_remote_copy(
             src_ref=src,
-            dst_ref=bank.at[me],
-            send_sem=send.at[k],
-            recv_sem=recv.at[k],
-            device_id={"member": lax.rem(me + k, n)},
+            dst_ref=bank.at[origin if arriving else me],
+            send_sem=send.at[j],
+            recv_sem=recv.at[j],
+            device_id={"member": to},
             device_id_type=pl.DeviceIdType.MESH,
         )
 
-    def member_arrival(src, bank, k, send, recv):
-        origin = lax.rem(me + n - k, n)
+    def inner_copy(src, bank, j, hop, send, recv, arriving=False):
+        from_outer = lax.rem(me_outer + outer - j, outer)
+        from_inner = lax.rem(me_inner + inner - hop, inner)
+        mine = from_outer * inner + me_inner
+        origin = from_outer * inner + from_inner
+        to = me_outer * inner + lax.rem(me_inner + hop, inner)
+        at = outer + j * (inner - 1) + hop - 1
         return pltpu.make_async_remote_copy(
-            src_ref=src,
-            dst_ref=bank.at[origin],
-            send_sem=send.at[k],
-            recv_sem=recv.at[k],
-            device_id={"member": lax.rem(me + k, n)},
+            src_ref=src if j == 0 else bank.at[mine],
+            dst_ref=bank.at[origin if arriving else mine],
+            send_sem=send.at[at],
+            recv_sem=recv.at[at],
+            device_id={"member": to},
             device_id_type=pl.DeviceIdType.MESH,
         )
+
+    hops = sorted(range(1, outer), key=lambda j: (min(j, outer - j), j))
+
+    def over_inner(do):
+        def step(hop, c):
+            do(hop)
+            return c
+
+        lax.fori_loop(1, inner, step, 0)
+
+    def gather_start(src, bank, send, recv):
+        over_inner(lambda hop: inner_copy(src, bank, 0, hop, send, recv).start())
+        for j in hops:
+            outer_copy(src, bank, j, send, recv).start()
+
+    def forward(src, bank, j, send, recv):
+        outer_copy(src, bank, j, send, recv, True).wait_recv()
+        over_inner(lambda hop: inner_copy(src, bank, j, hop, send, recv).start())
+
+    def gather_inner(src, bank, j, send, recv, use):
+        def do(hop):
+            inner_copy(src, bank, j, hop, send, recv, True).wait_recv()
+            from_outer = lax.rem(me_outer + outer - j, outer)
+            use(from_outer * inner + lax.rem(me_inner + inner - hop, inner))
+
+        over_inner(do)
+
+    def outer_origin(j):
+        return lax.rem(me_outer + outer - j, outer) * inner + me_inner
+
+    def gather_drain(src, bank, send, recv):
+        for j in hops:
+            outer_copy(src, bank, j, send, recv).wait_send()
+        for j in range(outer):
+            over_inner(lambda hop: inner_copy(src, bank, j, hop, send, recv).wait_send())
 
     def group_copy(bank, got, k, send, recv):
         to = lax.rem(g + k, groups)
@@ -122,20 +175,50 @@
         )
     pl.semaphore_wait(barrier, n - 1 + groups - 1)
 
-    def send_features(k, c):
-        member_copy(feat_ref, gather1, k, ag1_send, ag1_recv).start()
-        return c
-
-    lax.fori_loop(1, n, send_features, 0)
+    ag1 = (feat_ref, gather1)
+    sem1 = (ag1_send, ag1_recv)
+    gather_start(*ag1, *sem1)
+
+    for e in range(groups):
+        shape = (cap * blocks, feat_ref.shape[1])
+        line = lax.broadcasted_iota(jnp.int32, shape, 0)
+        value = jnp.zeros(shape, F32)
+        for c in range(cap):
+            target = jnp.where(c < count_ref[0, e], c * blocks + mirror_ref[0, e, c], -1)
+            value = jnp.where(line == target, 1.0, value)
+        hot_ref[e] = value
     for k in range(1, groups):
         group_copy(hot_ref, got_hot, k, hot_send, hot_recv).start()
 
-    gather1[me] = feat_ref[...]
+    slot = slot_ref[...]
+    dest = slot // cap
+    live = jnp.zeros(slot.shape, jnp.int32)
+    for e in range(groups):
+        live = jnp.where(dest == e, count_ref[0, e], live)
+    key = jnp.where(slot - dest * cap < live, slot * columns + column_ref[...], -1)
+    key_down = jnp.transpose(jnp.broadcast_to(key, (8, total)))[:, 0:1]
+    earlier = lax.broadcasted_iota(jnp.int32, (total, total), 0)
+    order = lax.broadcasted_iota(jnp.int32, (total, total), 1)
+    same = (key_down == key) & (earlier < order)
+    found = jnp.max(jnp.where(same, earlier, -1), axis=0, keepdims=True)
+    prev_vmem[...] = jnp.where(found < 0, total, found)
+    for i in range(0, slots * columns, total):
+        found = jnp.max(
+            jnp.where(key_down == order + i, earlier, -1), axis=0, keepdims=True
+        )
+        last_vmem[:, i : i + total] = jnp.where(found < 0, total, found)
+    prev_copy = pltpu.make_async_copy(prev_vmem, prev_ref, table_sem.at[0])
+    last_copy = pltpu.make_async_copy(last_vmem, last_ref, table_sem.at[1])
+    prev_copy.start()
+    last_copy.start()
     tile_buf[total] = jnp.zeros((size, size), BF16)
     run_buf[total] = jnp.zeros((size, size), F32)
 
+    prev_copy.wait()
+    last_copy.wait()
+
     def chain(t, c):
-        value = tile_buf[t].astype(F32) + run_buf[prev_ref[t]]
+        value = tile_buf[t].astype(F32) + run_buf[prev_ref[0, t]]
         run_buf[t] = value
         tile_buf[t] = value.astype(BF16)
         return c
@@ -143,13 +226,16 @@
     for i in range(pieces):
         tile_copy(i).wait()
         lax.fori_loop(i * piece, (i + 1) * piece, chain, 0)
-
-    def stage(k, at):
-        origin = lax.rem(me + n - k, n)
+        if i % 2 == 1 and i // 2 < len(hops):
+            forward(*ag1, hops[i // 2], *sem1)
+    for j in hops[pieces // 2 :]:
+        forward(*ag1, j, *sem1)
+
+    def stage(origin, at):
         for s in range(slots):
             for b in range(blocks):
                 stage_buf[at, s * size : (s + 1) * size, b * size : (b + 1) * size] = tile_buf[
-                    last_ref[s * columns + origin * blocks + b]
+                    last_ref[0, s * columns + origin * blocks + b]
                 ]
 
     if keep:
@@ -160,10 +246,10 @@
 
         lax.fori_loop(0, n, stage_all, 0)
 
-    def place(k):
+    def place(origin):
         if keep:
-            return k
-        stage(k, 0)
+            return origin
+        stage(origin, 0)
         return 0
 
     def combine(part, got):
@@ -187,16 +273,16 @@
             sums.append(value.astype(BF16))
         return sums
 
-    acc1[...] = jnp.dot(stage_buf[place(0)], feat_ref[...], preferred_element_type=F32)
-
-    def first_layer(k, c):
-        at = place(k)
-        member_arrival(feat_ref, gather1, k, ag1_send, ag1_recv).wait_recv()
-        origin = lax.rem(me + n - k, n)
+    acc1[...] = jnp.dot(stage_buf[place(me)], feat_ref[...], preferred_element_type=F32)
+
+    def first_layer(origin):
+        at = place(origin)
         acc1[...] += jnp.dot(stage_buf[at], gather1[origin], preferred_element_type=F32)
-        return c
-
-    lax.fori_loop(1, n, first_layer, 0)
+
+    for j in hops:
+        first_layer(outer_origin(j))
+    for j in [0] + hops:
+        gather_inner(*ag1, j, *sem1, first_layer)
     for e in range(groups):
         part1[e] = acc1[e * cap * size : (e + 1) * cap * size, :].astype(BF16)
     for k in range(1, groups):
@@ -209,39 +295,41 @@
     for b in range(blocks):
         own_sum[b * size : (b + 1) * size, :] = sums[b]
 
-    def send_sums(k, c):
-        member_copy(own_sum, gather2, k, ag2_send, ag2_recv).start()
-        return c
-
-    lax.fori_loop(1, n, send_sums, 0)
+    ag2 = (own_sum, gather2)
+    sem2 = (ag2_send, ag2_recv)
+    gather_start(*ag2, *sem2)
 
     def hidden_of(value):
         raw = jnp.dot(value, w1_ref[...], preferred_element_type=F32) + b1_ref[...]
         return jnp.maximum(raw, 0.0).astype(BF16)
 
-    acc2[...] = jnp.dot(stage_buf[place(0)], hidden_of(own_sum[...]), preferred_element_type=F32)
-
-    def second_layer(k, c):
-        at = place(k)
-        member_arrival(own_sum, gather2, k, ag2_send, ag2_recv).wait_recv()
-        origin = lax.rem(me + n - k, n)
+    acc2[...] = jnp.dot(stage_buf[place(me)], hidden_of(own_sum[...]), preferred_element_type=F32)
+
+    def second_layer(origin):
+        at = place(origin)
         acc2[...] += jnp.dot(
             stage_buf[at], hidden_of(gather2[origin]), preferred_element_type=F32
         )
-        return c
-
-    lax.fori_loop(1, n, second_layer, 0)
+
+    waiting = []
+    for j in hops:
+        forward(*ag2, j, *sem2)
+        for i in waiting:
+            second_layer(outer_origin(i))
+        waiting = [j]
+        if j == hops[1]:
+            gather_inner(*ag2, 0, *sem2, second_layer)
+    for i in waiting:
+        second_layer(outer_origin(i))
+    for j in hops:
+        gather_inner(*ag2, j, *sem2, second_layer)
     for e in range(groups):
         part2[e] = acc2[e * cap * size : (e + 1) * cap * size, :].astype(BF16)
     for k in range(1, groups):
         group_copy(part2, got2, k, rs2_send, rs2_recv).start()
 
-    def drain(k, c):
-        member_copy(feat_ref, gather1, k, ag1_send, ag1_recv).wait_send()
-        member_copy(own_sum, gather2, k, ag2_send, ag2_recv).wait_send()
-        return c
-
-    lax.fori_loop(1, n, drain, 0)
+    gather_drain(*ag1, *sem1)
+    gather_drain(*ag2, *sem2)
     for k in range(1, groups):
         group_copy(hot_ref, got_hot, k, hot_send, hot_recv).wait_send()
         group_copy(part1, got1, k, rs1_send, rs1_recv).wait_send()
@@ -277,36 +365,17 @@
     cap = mirror_block.shape[2]
     slots = groups * cap
     columns = n * blocks
-    counts = mirror_count[0]
-    slot = tile_slot[0]
-    dest = slot // cap
-    count_of = jnp.sum(
-        jnp.where(dest[:, None] == jnp.arange(groups)[None, :], counts[None, :], 0), axis=1
-    )
-    live = (slot % cap) < count_of
-    key = jnp.where(live, slot * columns + tile_column[0], -1)
-    order = jnp.arange(total, dtype=jnp.int32)
-    same = (key[:, None] == key[None, :]) & (order[None, :] < order[:, None])
-    prev = jnp.max(jnp.where(same, order[None, :], -1), axis=1)
-    prev = jnp.where(prev < 0, total, prev)
-    combos = jnp.arange(slots * columns, dtype=jnp.int32)
-    last = jnp.max(jnp.where(key[None, :] == combos[:, None], order[None, :], -1), axis=1)
-    last = jnp.where(last < 0, total, last)
-    hot = (mirror_block[0][:, :, None] == jnp.arange(blocks)[None, None, :]) & (
-        jnp.arange(cap)[None, :, None] < counts[:, None, None]
-    )
-    hot = jnp.broadcast_to(
-        hot.reshape(groups, cap * blocks, 1).astype(F32), (groups, cap * blocks, width)
-    )
     keep = slots * columns <= 2 * total
     pieces = 8 if total % 8 == 0 else 1
+    outer = 4
+    inner = n // outer
     vmem = pl.BlockSpec(memory_space=pltpu.VMEM)
     smem = pl.BlockSpec(memory_space=pltpu.SMEM)
     dma = pltpu.SemaphoreType.DMA
     return pl.pallas_call(
-        functools.partial(kernel, n, groups, cap, keep),
+        functools.partial(kernel, outer, inner, groups, cap, keep),
         out_shape=jax.ShapeDtypeStruct((rows, outs), BF16),
-        in_specs=[smem, smem, vmem, pl.BlockSpec(memory_space=pl.ANY)] + [vmem] * 5,
+        in_specs=[vmem, vmem, smem, smem, vmem, pl.BlockSpec(memory_space=pl.ANY)] + [vmem] * 4,
         out_specs=vmem,
         scratch_shapes=[
             pltpu.VMEM((total + 1, size, size), BF16),
@@ -322,6 +391,12 @@
             pltpu.VMEM((groups, cap * size, hidden), BF16),
             pltpu.VMEM((groups, cap * blocks, width), F32),
             pltpu.VMEM((rows, width), BF16),
+            pltpu.VMEM((groups, cap * blocks, width), F32),
+            pltpu.VMEM((1, total), jnp.int32),
+            pltpu.VMEM((1, slots * columns), jnp.int32),
+            pltpu.SMEM((1, total), jnp.int32),
+            pltpu.SMEM((1, slots * columns), jnp.int32),
+            dma((2,)),
             dma((pieces,)),
             dma((groups,)),
             dma((groups,)),
@@ -338,11 +413,12 @@
             collective_id=0, has_side_effects=True, vmem_limit_bytes=56 * 1024 * 1024
         ),
     )(
-        prev,
-        last,
+        tile_slot,
+        tile_column,
+        mirror_count,
+        mirror_block,
         features,
         edge_tiles,
-        hot,
         weight_first,
         bias_first.reshape(1, -1),
         weight_second,

time: 77 us -> 60.9 us (0.79)
  Pallas kernels: 69 us -> 57.5 us
  other arithmetic: 4.3 us -> 0 us
    pallas_call x1, Pallas kernels: 69 us -> 57.5 us  [body(): pl.pallas_call(functools.partial(kernel, outer, inner, groups, cap, keep)...]
    select_n x4 -> x0, other arithmetic: 2.69 us -> none  [the longest x2 1.41 us: body(): key = jnp.where(live, slot * columns + tile_column[0], -1)]
    unnamed x1 -> x2, local copies, waits for them, and re-layouts: 1.67 us -> 3.01 us
    eq x5 -> x0, local copies, waits for them, and re-layouts: 1.01 us -> none  [body(): mirror_block[0][:, :, None] == jnp.arange(blocks)[None, None, :]]
where the time goes in v2:
time: 60.9 us; the launch traced here: 60.5 us
  Pallas kernels  57.5 us (94%)
  local copies, waits for them, and re-layouts  3.01 us (5%)
    pallas_call x1, Pallas kernels, body(): pl.pallas_call(functools.partial(kernel, outer, inner, groups, cap, keep)...  57.5 us
    unnamed x2, local copies, waits for them, and re-layouts  3.01 us

profile of v2, /device:TPU:31, one launch (start us, length us, event | category | flops | bytes accessed | tf_op | source)
XLA Modules:
  0.0 60.5 jit_solution(2929414224661570167)
XLA Ops:
  0.0 1.3 %copy.11.mirror_ref = s32[1,4,2]{2,1,0:T(4,128)} copy(s32[1,4,2]{1,2,0:T(2,128)} %param.15) | data formatting | bytes 64 | tf_op args[5]
  1.3 57.5 %shard_map.100 = bf16[512,256]{1,0:T(8,128)(2,1)} custom-call(s32[1,256]{1,0:T(1,128)} %slot_ref.1, s32[1,256]{1,0:T(1,128)} %column_ref.1, s32[1,4]{1,0:T(1,128)} %count_ref.1, s32[1,4,2]{2,1,0:T(4,128)} %copy.11.mirror_ref, bf16[512,128]{1,0:T(8,128)(2,1)} %feat_ref.1, bf16[256,128,128]{2,1,0:T(8,128)(2,1)} %tiles_ref.1, bf16[128,256]{1,0:T(8,128)(2,1)} %w1_ref.1, ...), custom_call_target="tpu_custom_call" | custom-call | tf_op jit(solution)/shard_map/pallas_call | solution.py:375
  58.8 1.7 %copy.13 = bf16[512,256]{1,0:T(8,128)(2,1)} copy(bf16[512,256]{1,0:T(8,128)(2,1)} %shard_map.100) | data formatting | bytes 524288

commit v3 on v2

--- a/solution.py
+++ b/solution.py
@@ -225,7 +225,7 @@
 
     for i in range(pieces):
         tile_copy(i).wait()
-        lax.fori_loop(i * piece, (i + 1) * piece, chain, 0)
+        lax.fori_loop(i * piece, (i + 1) * piece, chain, 0, unroll=4)
         if i % 2 == 1 and i // 2 < len(hops):
             forward(*ag1, hops[i // 2], *sem1)
     for j in hops[pieces // 2 :]:

time: 60.9 us -> 59.9 us (0.984)
  Pallas kernels: 57.5 us -> 56.7 us
    pallas_call x1, Pallas kernels: 57.5 us -> 56.7 us  [body(): pl.pallas_call(functools.partial(kernel, outer, inner, groups, cap, keep)...]
where the time goes in v3:
time: 59.9 us; the launch traced here: 59.7 us
  Pallas kernels  56.7 us (95%)
  local copies, waits for them, and re-layouts  3.01 us (5%)
    pallas_call x1, Pallas kernels, body(): pl.pallas_call(functools.partial(kernel, outer, inner, groups, cap, keep)...  56.7 us
    unnamed x2, local copies, waits for them, and re-layouts  3.01 us

profile of v3, /device:TPU:31, one launch (start us, length us, event | category | flops | bytes accessed | tf_op | source)
XLA Modules:
  0.0 59.7 jit_solution(13244752985585238995)
XLA Ops:
  0.0 1.3 %copy.11.mirror_ref = s32[1,4,2]{2,1,0:T(4,128)} copy(s32[1,4,2]{1,2,0:T(2,128)} %param.15) | data formatting | bytes 64 | tf_op args[5]
  1.3 56.7 %shard_map.100 = bf16[512,256]{1,0:T(8,128)(2,1)} custom-call(s32[1,256]{1,0:T(1,128)} %slot_ref.1, s32[1,256]{1,0:T(1,128)} %column_ref.1, s32[1,4]{1,0:T(1,128)} %count_ref.1, s32[1,4,2]{2,1,0:T(4,128)} %copy.11.mirror_ref, bf16[512,128]{1,0:T(8,128)(2,1)} %feat_ref.1, bf16[256,128,128]{2,1,0:T(8,128)(2,1)} %tiles_ref.1, bf16[128,256]{1,0:T(8,128)(2,1)} %w1_ref.1, ...), custom_call_target="tpu_custom_call" | custom-call | tf_op jit(solution)/shard_map/pallas_call | solution.py:375
  58.0 1.7 %copy.13 = bf16[512,256]{1,0:T(8,128)(2,1)} copy(bf16[512,256]{1,0:T(8,128)(2,1)} %shard_map.100) | data formatting | bytes 524288
